TPU v7x, 32 devices: a whole 2x2x4 slice. The times are simulated.
32 devices in a mesh: seq: 8 (over z, y), head: 4 (over x, core).
Axes of the slice: x: 2, y: 2, z: 4, core: 2. Of those that a mesh axis runs over, the one named last changes fastest.
Arguments:
- queries: bfloat16 [4096, 2048], P('seq', 'head'), may hold values from -6 to 6
- keys: bfloat16 [4096, 2048], P('seq', 'head'), may hold values from -6 to 6
- values: bfloat16 [4096, 2048], P('seq', 'head'), may hold values from -6 to 6
- level_weights: int32 [16, 20], P('head'), may hold values from 1 to 8
- out_grad: bfloat16 [4096, 2048], P('seq'), may hold values from -6 to 6
Outputs:
- normed: bfloat16 [4096, 2048], P('seq', 'head')
- proj_grad: float32 [2048, 2048], P('seq', 'head')
All inputs are finite; a program needn't handle non-finite values.
Results may differ from a plain program's by a relative error of at most 0.0031.
Values sent between devices are 32-bit elements; how exact they have to be, the bound alone decides.
A program may use at most 64 MiB of HBM per device.

v0:
```python
import jax
import jax.numpy as jnp
from jax import lax
from jax.sharding import PartitionSpec as P

D = 2048
HEADS = 16
GROUP = 512
LEVELS = 20


def partner_2(block, axis, bit):
    count = lax.axis_size(axis)
    route = []
    for low in range(count):
        high = low | 1 << bit
        if high != low and high < count:
            route += [(low, high), (high, low)]
    return lax.ppermute(block, axis, route)


def count_levels(mixed):
    level = jnp.zeros(mixed.shape, jnp.int32)
    for bit in range(LEVELS):
        level = level + (mixed >= 2**bit).astype(jnp.int32)
    return level


def body(queries, keys, values, level_weights, out_grad):
    tok_rows, width = queries.shape
    head_dim = D // HEADS
    heads_here = width // head_dim
    per_dev = tok_rows // GROUP
    local_bits = per_dev.bit_length() - 1
    scale = head_dim ** (-0.5)
    q_blocks = queries.reshape(per_dev, GROUP, heads_here, head_dim)
    k_blocks = keys.reshape(per_dev, GROUP, heads_here, head_dim)
    v_blocks = values.reshape(per_dev, GROUP, heads_here, head_dim)
    weights = level_weights.astype(jnp.float32)
    level_ids = jnp.arange(LEVELS, dtype=jnp.int32)
    state = jnp.einsum("cnhd,cnhe->chde", k_blocks, v_blocks, preferred_element_type=jnp.float32)
    own_state = jnp.sum(state, axis=0)
    local_index = jnp.arange(per_dev, dtype=jnp.int32)
    local_level = count_levels(jnp.bitwise_xor(local_index[:, None], local_index[None, :]))
    earlier = (local_index[None, :] < local_index[:, None]).astype(jnp.float32)
    picker = (local_level[:, :, None] == level_ids[None, None, :]).astype(jnp.float32) * earlier[
        :, :, None
    ]
    local_table = jnp.einsum("cjl,hl->hcj", picker, weights, precision=lax.Precision.HIGHEST)
    mix = jnp.einsum("hcj,jhde->chde", local_table, state, precision=lax.Precision.HIGHEST)
    position = lax.axis_index("seq")
    nbits = lax.axis_size("seq").bit_length() - 1
    block = own_state
    remote = jnp.zeros_like(own_state)
    for bit in range(nbits):
        partner = partner_2(block, "seq", bit)
        upper = jnp.right_shift(position, bit) % 2
        level_weight = weights[:, local_bits + 1 + bit] * upper.astype(jnp.float32)
        remote = remote + level_weight[:, None, None] * partner
        block = block + partner
    mix = mix + remote[None]
    far = scale * jnp.einsum(
        "cnhd,chde->cnhe", q_blocks.astype(jnp.float32), mix, precision=lax.Precision.HIGHEST
    )
    scores = jnp.einsum("cnhd,cmhd->chnm", q_blocks, k_blocks, preferred_element_type=jnp.float32)
    scores = scores * (scale * weights[:, 0])[None, :, None, None]
    rows = jnp.arange(GROUP, dtype=jnp.int32)
    causal = rows[None, :] <= rows[:, None]
    probs = jnp.where(causal[None, None], scores, 0.0).astype(jnp.bfloat16)
    near = jnp.einsum("chnm,cmhe->cnhe", probs, v_blocks, preferred_element_type=jnp.float32)
    raw = (near + far).reshape(tok_rows, width)
    row_squares = lax.psum(jnp.sum(raw * raw, axis=1), "head")
    normed = (raw * lax.rsqrt(row_squares / D + 1e-06)[:, None]).astype(jnp.bfloat16)
    dims = (((0,), (0,)), ((), ()))
    whole_term = lax.dot_general(out_grad, normed, dims, preferred_element_type=jnp.float32)
    proj_grad = lax.psum_scatter(whole_term, "seq", scatter_dimension=0, tiled=True)
    return (normed, proj_grad)


def solution(mesh):
    return jax.shard_map(
        body,
        mesh=mesh,
        in_specs=(
            P("seq", "head"),
            P("seq", "head"),
            P("seq", "head"),
            P("head", None),
            P("seq", None),
        ),
        out_specs=(P("seq", "head"), P("seq", "head")),
        check_vma=False,
    )
```

profile of v0, /device:TPU:0, one launch (start us, length us, event | category | flops | bytes accessed | tf_op | source)
XLA Modules:
  0.0 156.3 jit_solution(1530813651230132948)
XLA Ops:
  7.2 0.0 copy-start
  7.2 0.0 reduce-scatter.2.cloned.1.call-start
  7.2 1.4 copy.15
  8.6 1.3 fusion.5
  10.0 3.1 %collective-permute-start = (f32[4,128,128]{2,1,0:T(8,128)S(1)}, f32[4,128,128]{2,1,0:T(8,128)S(1)}, u32[]{:S(2)}, u32[]{:S(2)}) collective-permute-start(f32[4,128,128]{2,1,0:T(8,128)S(1)} %fusion.5), channel_id=1, source_target_pairs={{0,4},{4,0},{8,12},{12,8},{16,20},{20,16},{24,28},{28,24},{1,5},{5... | collective-permute-start | bytes 786440 | tf_op jit(solution)/shard_map/ppermute | solution.py:19
  13.0 6.3 %collective-permute-done = f32[4,128,128]{2,1,0:T(8,128)S(1)} collective-permute-done((f32[4,128,128]{2,1,0:T(8,128)S(1)}, f32[4,128,128]{2,1,0:T(8,128)S(1)}, u32[]{:S(2)}, u32[]{:S(2)}) %collective-permute-start) | collective-permute-done | bytes 262176 | tf_op jit(solution)/shard_map/ppermute | solution.py:19
  19.3 0.7 add.47
  20.1 1.8 %collective-permute-start.1 = (f32[4,128,128]{2,1,0:T(8,128)}, f32[4,128,128]{2,1,0:T(8,128)S(1)}, u32[]{:S(2)}, u32[]{:S(2)}) collective-permute-start(f32[4,128,128]{2,1,0:T(8,128)} %add.47), channel_id=1, source_target_pairs={{0,8},{8,0},{4,12},{12,4},{16,24},{24,16},{20,28},{28,20},{1,9},{9... | collective-permute-start | bytes 786440 | tf_op jit(solution)/shard_map/ppermute | solution.py:19
  21.9 0.8 convolution_bitcast_fusion.1
  22.7 0.7 convert_element_type.21
  23.4 0.2 multiply_reduce_fusion.2
  23.6 0.8 iota_compare_fusion
  24.4 3.4 %collective-permute-done.1 = f32[4,128,128]{2,1,0:T(8,128)S(1)} collective-permute-done((f32[4,128,128]{2,1,0:T(8,128)}, f32[4,128,128]{2,1,0:T(8,128)S(1)}, u32[]{:S(2)}, u32[]{:S(2)}) %collective-permute-start.1) | collective-permute-done | bytes 262176 | tf_op jit(solution)/shard_map/ppermute | solution.py:19
  27.7 1.7 %add.50 = f32[4,128,128]{2,1,0:T(8,128)} add(f32[4,128,128]{2,1,0:T(8,128)} %add.47, f32[4,128,128]{2,1,0:T(8,128)S(1)} %collective-permute-done.1) | non-fusion elementwise | flops 65536 | bytes 786432 | tf_op jit(solution)/shard_map/add | solution.py:60
  29.4 2.5 %collective-permute-start.2 = (f32[4,128,128]{2,1,0:T(8,128)}, f32[4,128,128]{2,1,0:T(8,128)}, u32[]{:S(2)}, u32[]{:S(2)}) collective-permute-start(f32[4,128,128]{2,1,0:T(8,128)} %add.50), channel_id=1, source_target_pairs={{0,16},{16,0},{4,20},{20,4},{8,24},{24,8},{12,28},{28,12},{1,17},{... | collective-permute-start | bytes 786440 | tf_op jit(solution)/shard_map/ppermute | solution.py:19
  32.0 3.6 %fusion.1 = f32[4,128,512]{2,1,0:T(8,128)} fusion(bf16[512,4,128]{0,2,1:T(8,128)(2,1)S(1)} %bitcast.49, f32[4]{0:T(128)S(1)} %get-tuple-element.7, pred[512,512]{1,0:T(8,128)(4,1)} %iota_compare_fusion, bf16[512,512]{1,0:T(8,128)(2,1)} %param.7, bf16[512,512]{1,0:T(8,128)(2,1)} %param.5), kind=kOutput, calls=%fused_computation.3 | convolution fusion | flops 540016640 | bytes 2883600 | tf_op jit(solution)/shard_map/chnm,cmhe->cnhe/dot_general | solution.py:70
  35.6 7.3 %collective-permute-done.2 = f32[4,128,128]{2,1,0:T(8,128)} collective-permute-done((f32[4,128,128]{2,1,0:T(8,128)}, f32[4,128,128]{2,1,0:T(8,128)}, u32[]{:S(2)}, u32[]{:S(2)}) %collective-permute-start.2) | collective-permute-done | bytes 262176 | tf_op jit(solution)/shard_map/ppermute | solution.py:19
  42.9 3.2 %fusion.3 = (f32[512]{0:T(512)S(1)}, f32[4,128,512]{2,1,0:T(8,128)}) fusion(f32[4,128,512]{2,1,0:T(8,128)} %fusion.1, f32[4,128,128]{2,1,0:T(8,128)} %collective-permute-done.2, f32[4,128,128]{2,1,0:T(8,128)S(1)} %collective-permute-done.1, f32[4,128,128]{2,1,0:T(8,128)S(1)} %collective-permute-done, f32[4,128,128]{2,1,0:T(8,128)S(1)} %fusion.5, ...), kind=kOutput, calls=%fused_computation.8 | convolution fusion | flops 404160000 | bytes 3672128 | tf_op jit(solution)/shard_map/cnhd,chde->cnhe/dot_general | solution.py:62
  46.1 5.6 %psum.7 = f32[512]{0:T(512)S(1)} all-reduce(f32[512]{0:T(512)S(1)} %get-tuple-element.8), channel_id=1, replica_groups=mesh['seq'=8,'head'=4] {'head'}, use_global_device_ids=true, to_apply=%region_1.2 | all-reduce | flops 512 | bytes 4096 | tf_op jit(solution)/shard_map/psum | solution.py:72
  51.7 1.6 copy.12
  53.3 0.1 multiply_convert_fusion
  53.4 0.0 copy-start.1
  53.5 0.8 copy-done.1
  54.2 0.0 copy-done
  54.2 3.2 %convolution_bitcast_fusion = f32[2048,512]{0,1:T(8,128)} fusion(bf16[512,512]{1,0:T(8,128)(2,1)S(1)} %multiply_convert_fusion, bf16[512,2048]{1,0:T(8,128)(2,1)S(1)} %copy-done), kind=kOutput, calls=%fused_computation.1 | convolution fusion | flops 1073741824 | bytes 6815744 | tf_op jit(solution)/shard_map/dot_general | solution.py:75
  57.5 0.0 reduce-scatter.2.cloned.1.call-update
  57.5 90.0 %reduce-scatter.2.cloned.1.call-done = f32[256,512]{0,1:T(8,128)} async-done(((f32[2048,512]{0,1:T(8,128)}), f32[256,512]{0,1:T(8,128)}) %reduce-scatter.2.cloned.1.call-update) | async-done | bytes 524304 | tf_op jit(solution)/shard_map/reduce_scatter | solution.py:76
  147.5 2.0 %copy.13 = f32[256,512]{1,0:T(8,128)} copy(f32[256,512]{0,1:T(8,128)} %reduce-scatter.2.cloned.1.call-done) | data formatting | bytes 1048576
  (1 shorter events, 0.0 us)
Async XLA Ops:
  7.2 47.1 %copy-start = (bf16[512,2048]{1,0:T(8,128)(2,1)S(1)}, bf16[512,2048]{1,0:T(8,128)(2,1)}, u32[]{:S(2)}) copy-start(bf16[512,2048]{1,0:T(8,128)(2,1)} %param.9) | copy-start | bytes 6291460
  7.2 140.3 %reduce-scatter.2.cloned.1.call-start = ((), (), s32[]{:S(2)}) async-start(), calls=%async_computation.1 | async-start | bytes 4718592 | tf_op jit(solution)/shard_map/reduce_scatter | solution.py:76
  10.0 9.4 %collective-permute-start = (f32[4,128,128]{2,1,0:T(8,128)S(1)}, f32[4,128,128]{2,1,0:T(8,128)S(1)}, u32[]{:S(2)}, u32[]{:S(2)}) collective-permute-start(f32[4,128,128]{2,1,0:T(8,128)S(1)} %fusion.5), channel_id=1, source_target_pairs={{0,4},{4,0},{8,12},{12,8},{16,20},{20,16},{24,28},{28,24},{1,5},{5... | collective-permute-start | bytes 786440 | tf_op jit(solution)/shard_map/ppermute | solution.py:19
  20.1 7.7 %collective-permute-start.1 = (f32[4,128,128]{2,1,0:T(8,128)}, f32[4,128,128]{2,1,0:T(8,128)S(1)}, u32[]{:S(2)}, u32[]{:S(2)}) collective-permute-start(f32[4,128,128]{2,1,0:T(8,128)} %add.47), channel_id=1, source_target_pairs={{0,8},{8,0},{4,12},{12,4},{16,24},{24,16},{20,28},{28,20},{1,9},{9... | collective-permute-start | bytes 786440 | tf_op jit(solution)/shard_map/ppermute | solution.py:19
  29.4 13.4 %collective-permute-start.2 = (f32[4,128,128]{2,1,0:T(8,128)}, f32[4,128,128]{2,1,0:T(8,128)}, u32[]{:S(2)}, u32[]{:S(2)}) collective-permute-start(f32[4,128,128]{2,1,0:T(8,128)} %add.50), channel_id=1, source_target_pairs={{0,16},{16,0},{4,20},{20,4},{8,24},{24,8},{12,28},{28,12},{1,17},{... | collective-permute-start | bytes 786440 | tf_op jit(solution)/shard_map/ppermute | solution.py:19
  53.4 0.8 copy-start.1
Sparse Core Ops, SparseCore 0:
  57.6 89.8 reduce-scatter.1
where the time goes:
time: 157 us; the launch traced here: 156 us
  waiting for transfers between devices  107 us (68%)
  between operations  14.1 us (9%)
  matrix products  12.2 us (8%)
  starting transfers between devices  7.43 us (5%)
  local copies, waits for them, and re-layouts  5.78 us (4%)
  blocking collectives  5.63 us (4%)
  other arithmetic  4.25 us (3%)
    reduce_scatter x1, waiting for transfers between devices, body(): lax.psum_scatter(whole_term, 'seq', scatter_dimension=0, tiled=True)  90 us
    ppermute x3, waiting for transfers between devices, partner_2(): return lax.ppermute(block, axis, route)  17 us
    ppermute x3, starting transfers between devices, partner_2(): return lax.ppermute(block, axis, route)  7.39 us
    psum x1, blocking collectives, body(): row_squares = lax.psum(jnp.sum(raw * raw, axis=1), 'head')  5.63 us
    dot_general x1, matrix products, body(): jnp.einsum('chnm,cmhe->cnhe', probs, v_blocks, preferred_element_type=jnp...  3.61 us
    dot_general x1, matrix products, body(): jnp.einsum('cnhd,chde->cnhe', q_blocks.astype(jnp.float32), mix, precisio...  3.22 us
    dot_general x1, matrix products, body(): lax.dot_general(out_grad, normed, dims, preferred_element_type=jnp.float32)  3.21 us
  transfers between devices with their start and end apart: 4, of which 4 were waited for; matrix products, arithmetic and copies ran while one was open for 4% of the time, Pallas kernels for 0%

commit v1 on v0

--- a/solution.py
+++ b/solution.py
@@ -1,12 +1,17 @@
+import functools
+
 import jax
 import jax.numpy as jnp
 from jax import lax
+from jax.experimental import pallas as pl
+from jax.experimental.pallas import tpu as pltpu
 from jax.sharding import PartitionSpec as P
 
 D = 2048
 HEADS = 16
 GROUP = 512
 LEVELS = 20
+MESH = pl.DeviceIdType.MESH
 
 
 def partner_2(block, axis, bit):
@@ -24,6 +29,209 @@
     for bit in range(LEVELS):
         level = level + (mixed >= 2**bit).astype(jnp.int32)
     return level
+
+
+def reduce_kernel(
+    line,
+    chunks,
+    lanes,
+    grad_ref,
+    theirs_ref,
+    normed_ref,
+    out_ref,
+    sent,
+    came,
+    part,
+    rising,
+    falling,
+    pair_send,
+    pair_recv,
+    up_send,
+    up_recv,
+    down_send,
+    down_recv,
+):
+    me = lax.axis_index("seq")
+    place = me // 2
+    side = me % 2
+    other = place * 2 + 1 - side
+    above = me + 2
+    below = me - 2
+    low_end = place == 0
+    high_end = place == line - 1
+    inner = jnp.logical_and(place > 0, place < line - 1)
+
+    barrier = pltpu.get_barrier_semaphore()
+    pl.semaphore_signal(barrier, inc=1, device_id={"seq": other}, device_id_type=MESH)
+
+    @pl.when(place < line - 1)
+    def _():
+        pl.semaphore_signal(barrier, inc=1, device_id={"seq": above}, device_id_type=MESH)
+
+    @pl.when(place > 0)
+    def _():
+        pl.semaphore_signal(barrier, inc=1, device_id={"seq": below}, device_id_type=MESH)
+
+    for k in range(chunks):
+        sent[k] = normed_ref[:, k * lanes : (k + 1) * lanes].astype(jnp.float32)
+
+    peers = 1 + jnp.where(place > 0, 1, 0) + jnp.where(place < line - 1, 1, 0)
+    pl.semaphore_wait(barrier, peers)
+
+    def pair_copy(k):
+        return pltpu.make_async_remote_copy(
+            src_ref=sent.at[k],
+            dst_ref=came.at[k],
+            send_sem=pair_send.at[k],
+            recv_sem=pair_recv.at[k],
+            device_id={"seq": other},
+            device_id_type=MESH,
+        )
+
+    def up_copy(k, d):
+        return pltpu.make_async_remote_copy(
+            src_ref=part.at[k, d],
+            dst_ref=rising.at[k, d],
+            send_sem=up_send.at[k, d],
+            recv_sem=up_recv.at[k, d],
+            device_id={"seq": above},
+            device_id_type=MESH,
+        )
+
+    def down_copy(k, d):
+        return pltpu.make_async_remote_copy(
+            src_ref=part.at[k, d],
+            dst_ref=falling.at[k, d],
+            send_sem=down_send.at[k, d],
+            recv_sem=down_recv.at[k, d],
+            device_id={"seq": below},
+            device_id_type=MESH,
+        )
+
+    for k in range(chunks):
+        pair_copy(k).start()
+
+    def ends(k):
+        @pl.when(low_end)
+        def _():
+            @pl.loop(0, line - 1)
+            def _(i):
+                up_copy(k, line - 1 - i).start()
+
+        @pl.when(high_end)
+        def _():
+            @pl.loop(0, line - 1)
+            def _(d):
+                down_copy(k, d).start()
+
+    def middle(k):
+        @pl.when(inner)
+        def _():
+            @pl.loop(0, line - 1 - place)
+            def _(i):
+                d = line - 1 - i
+                up_copy(k, d).wait_recv()
+                part[k, d] = part[k, d] + rising[k, d]
+                up_copy(k, d).start()
+
+            @pl.loop(0, place)
+            def _(d):
+                down_copy(k, d).wait_recv()
+                part[k, d] = part[k, d] + falling[k, d]
+                down_copy(k, d).start()
+
+    theirs = theirs_ref[...].astype(jnp.bfloat16)
+    for k in range(chunks):
+        pair_copy(k).wait_recv()
+        here = normed_ref[:, k * lanes : (k + 1) * lanes]
+        there = came[k].astype(jnp.bfloat16)
+        total = jnp.dot(grad_ref[...], here, preferred_element_type=jnp.float32)
+        total = total + jnp.dot(theirs, there, preferred_element_type=jnp.float32)
+        part[k] = total.reshape(part.shape[1:])
+        ends(k)
+        if k:
+            middle(k - 1)
+    middle(chunks - 1)
+
+    for k in range(chunks):
+        span = slice(k * lanes, (k + 1) * lanes)
+        out_ref[:, span] = part[k, place]
+
+        @pl.when(place > 0)
+        def _():
+            up_copy(k, place).wait_recv()
+            out_ref[:, span] = out_ref[:, span] + rising[k, place]
+
+        @pl.when(place < line - 1)
+        def _():
+            down_copy(k, place).wait_recv()
+            out_ref[:, span] = out_ref[:, span] + falling[k, place]
+
+    for k in range(chunks):
+        pair_copy(k).wait_send()
+
+        @pl.loop(place + 1, line)
+        def _(d):
+            up_copy(k, d).wait_send()
+
+        @pl.loop(0, place)
+        def _(d):
+            down_copy(k, d).wait_send()
+
+
+def weight_grad(grads, theirs, normed):
+    tokens, width = normed.shape
+    line = lax.axis_size("seq") // 2
+    lanes = D // HEADS
+    chunks = width // lanes
+    rows = grads.shape[0] // line
+    slots = (chunks, line, rows, lanes)
+    vmem = pl.BlockSpec(memory_space=pltpu.VMEM)
+    return pl.pallas_call(
+        functools.partial(reduce_kernel, line, chunks, lanes),
+        out_shape=jax.ShapeDtypeStruct((rows, width), jnp.float32),
+        in_specs=[vmem, vmem, vmem],
+        out_specs=vmem,
+        scratch_shapes=[
+            pltpu.VMEM((chunks, tokens, lanes), jnp.float32),
+            pltpu.VMEM((chunks, tokens, lanes), jnp.float32),
+            pltpu.VMEM(slots, jnp.float32),
+            pltpu.VMEM(slots, jnp.float32),
+            pltpu.VMEM(slots, jnp.float32),
+            pltpu.SemaphoreType.DMA((chunks,)),
+            pltpu.SemaphoreType.DMA((chunks,)),
+            pltpu.SemaphoreType.DMA((chunks, line)),
+            pltpu.SemaphoreType.DMA((chunks, line)),
+            pltpu.SemaphoreType.DMA((chunks, line)),
+            pltpu.SemaphoreType.DMA((chunks, line)),
+        ],
+        compiler_params=pltpu.CompilerParams(
+            collective_id=0, has_side_effects=True, vmem_limit_bytes=40 << 20
+        ),
+    )(grads, theirs, normed)
+
+
+def exchange_grads(out_grad):
+    tokens = out_grad.shape[0]
+    count = lax.axis_size("seq")
+    heads = lax.axis_size("head")
+    line = count // 2
+    side = lax.axis_index("seq") % 2
+    head = lax.axis_index("head")
+    by_side = lax.optimization_barrier(out_grad.T).reshape(line, 2, D // count, tokens)
+    mine = lax.dynamic_index_in_dim(by_side, side, 1, keepdims=False).reshape(D // 2, tokens)
+    theirs = lax.dynamic_index_in_dim(by_side, 1 - side, 1, keepdims=False).reshape(D // 2, tokens)
+    piece = tokens // heads
+    block = lax.dynamic_slice_in_dim(theirs, head * piece, piece, 1).astype(jnp.float32)
+    blocks = [partner_2(block, "seq", 0)]
+    owners = [head]
+    for bit in reversed(range(heads.bit_length() - 1)):
+        blocks += [partner_2(block, "head", bit) for block in blocks]
+        owners += [jnp.bitwise_xor(owner, 1 << bit) for owner in owners]
+    gathered = jnp.zeros((D // 2, tokens), jnp.float32)
+    for block, owner in zip(blocks, owners):
+        gathered = lax.dynamic_update_slice_in_dim(gathered, block, owner * piece, 1)
+    return mine, gathered
 
 
 def body(queries, keys, values, level_weights, out_grad):
@@ -50,6 +258,7 @@
     mix = jnp.einsum("hcj,jhde->chde", local_table, state, precision=lax.Precision.HIGHEST)
     position = lax.axis_index("seq")
     nbits = lax.axis_size("seq").bit_length() - 1
+    grads, theirs = exchange_grads(out_grad)
     block = own_state
     remote = jnp.zeros_like(own_state)
     for bit in range(nbits):
@@ -71,9 +280,7 @@
     raw = (near + far).reshape(tok_rows, width)
     row_squares = lax.psum(jnp.sum(raw * raw, axis=1), "head")
     normed = (raw * lax.rsqrt(row_squares / D + 1e-06)[:, None]).astype(jnp.bfloat16)
-    dims = (((0,), (0,)), ((), ()))
-    whole_term = lax.dot_general(out_grad, normed, dims, preferred_element_type=jnp.float32)
-    proj_grad = lax.psum_scatter(whole_term, "seq", scatter_dimension=0, tiled=True)
+    proj_grad = weight_grad(grads, theirs, normed)
     return (normed, proj_grad)
 
 

time: 157 us -> 121 us (0.77)
  waiting for transfers between devices: 107 us -> 4.17 us
  Pallas kernels: 0 us -> 56.9 us
  local copies, waits for them, and re-layouts: 5.78 us -> 26.9 us
  between operations: 14.1 us -> 0.82 us
  matrix products: 12.2 us -> 7.86 us
  blocking collectives: 5.63 us -> 9.13 us
  starting transfers between devices: 7.43 us -> 9.41 us
    reduce_scatter x1 -> x0, waiting for transfers between devices: 90 us -> none  [body(): lax.psum_scatter(whole_term, 'seq', scatter_dimension=0, tiled=True)]
    pallas_call x0 -> x1, Pallas kernels: none -> 56.9 us  [weight_grad(): pl.pallas_call(functools.partial(reduce_kernel, line, chunks, lanes), out...]
    ppermute x3 -> x7, waiting for transfers between devices: 17 us -> 4.17 us  [partner_2(): return lax.ppermute(block, axis, route)]
    unnamed x5 -> x19, local copies, waits for them, and re-layouts: 2.83 us -> 9.64 us
    dynamic_slice x0 -> x1, local copies, waits for them, and re-layouts: none -> 6.34 us  [exchange_grads(): lax.dynamic_index_in_dim(by_side, 1 - side, 1, keepdims=False)]
    dynamic_update_slice x0 -> x4, local copies, waits for them, and re-layouts: none -> 3.58 us  [exchange_grads(): lax.dynamic_update_slice_in_dim(gathered, block, owner * piece, 1)]
    psum x1, blocking collectives: 5.63 us -> 9.13 us  [body(): row_squares = lax.psum(jnp.sum(raw * raw, axis=1), 'head')]
    reshape x0 -> x1, local copies, waits for them, and re-layouts: none -> 3.29 us  [exchange_grads(): lax.optimization_barrier(out_grad.T).reshape(line, 2, D // count, tokens)]
  transfers between devices with their start and end apart: 4 -> 7, of which waited for: 4 -> 2; matrix products, arithmetic and copies ran while one was open for 4% -> 29% of each run, Pallas kernels for 0% -> 0%
where the time goes in v1:
time: 121 us; the launch traced here: 120 us
  Pallas kernels  56.9 us (47%)
  local copies, waits for them, and re-layouts  26.9 us (22%)
  starting transfers between devices  9.41 us (8%)
  blocking collectives  9.13 us (8%)
  matrix products  7.86 us (6%)
  other arithmetic  5.06 us (4%)
  waiting for transfers between devices  4.17 us (3%)
    pallas_call x1, Pallas kernels, weight_grad(): pl.pallas_call(functools.partial(reduce_kernel, line, chunks, lanes), out...  56.9 us
    unnamed x19, local copies, waits for them, and re-layouts  9.64 us
    ppermute x7, starting transfers between devices, partner_2(): return lax.ppermute(block, axis, route)  9.41 us
    psum x1, blocking collectives, body(): row_squares = lax.psum(jnp.sum(raw * raw, axis=1), 'head')  9.13 us
    dynamic_slice x1, local copies, waits for them, and re-layouts, exchange_grads(): lax.dynamic_index_in_dim(by_side, 1 - side, 1, keepdims=False)  6.34 us
    ppermute x7, waiting for transfers between devices, partner_2(): return lax.ppermute(block, axis, route)  4.17 us
    dot_general x1, matrix products, body(): jnp.einsum('chnm,cmhe->cnhe', probs, v_blocks, preferred_element_type=jnp...  3.62 us
    dynamic_update_slice x4, local copies, waits for them, and re-layouts, exchange_grads(): lax.dynamic_update_slice_in_dim(gathered, block, owner * piece, 1)  3.58 us
  transfers between devices with their start and end apart: 7, of which 2 were waited for; matrix products, arithmetic and copies ran while one was open for 29% of the time, Pallas kernels for 0%

profile of v1, /device:TPU:0, one launch (start us, length us, event | category | flops | bytes accessed | tf_op | source)
XLA Modules:
  0.0 120.3 jit_solution(12849779379543816603)
XLA Ops:
  0.6 1.3 %copy.16 = bf16[512,512]{0,1:T(8,128)(2,1)S(1)} copy(bf16[512,512]{1,0:T(8,128)(2,1)} %param.6) | data formatting | bytes 1048576 | tf_op jit(solution)/shard_map/reshape.2
  2.0 1.3 %fusion.5 = f32[4,128,128]{2,1,0:T(8,128)S(1)} fusion(bf16[512,4,128]{0,2,1:T(8,128)(2,1)S(1)} %bitcast.51, bf16[512,512]{1,0:T(8,128)(2,1)} %param.7), kind=kOutput, calls=%fused_computation.11 | convolution fusion | flops 67108864 | bytes 1310720 | tf_op jit(solution)/shard_map/cnhd,cnhe->chde/dot_general | solution.py:249
  3.3 3.1 %collective-permute-start = (f32[4,128,128]{2,1,0:T(8,128)S(1)}, f32[4,128,128]{2,1,0:T(8,128)}, u32[]{:S(2)}, u32[]{:S(2)}) collective-permute-start(f32[4,128,128]{2,1,0:T(8,128)S(1)} %fusion.5), channel_id=1, source_target_pairs={{0,4},{4,0},{8,12},{12,8},{16,20},{20,16},{24,28},{28,24},{1,5},{5... | collective-permute-start | bytes 786440 | tf_op jit(solution)/shard_map/ppermute | solution.py:24
  6.4 3.3 %reshape.119 = bf16[4,2,256,512]{2,1,0,3:T(2,128)(2,1)S(1)} reshape(bf16[2048,512]{0,1:T(8,128)(2,1)} %bitcast.50) | data formatting | bytes 4194304 | tf_op jit(solution)/shard_map/reshape | solution.py:221
  9.7 6.3 %constant_dynamic-slice_fusion = (bf16[4,1,256,512]{2,1,0,3:T(2,128)(2,1)}, bf16[4,1,256,512]{2,1,0,3:T(2,128)(2,1)}) fusion(bf16[4,2,256,512]{2,1,0,3:T(2,128)(2,1)S(1)} %reshape.119, s32[]{:T(128)S(6)} %select_n.50, s32[]{:T(128)S(6)} %select_n.49), kind=kLoop, calls=%fused_computation.40 | loop fusion | bytes 4194312 | tf_op jit(solution)/shard_map/jit(dynamic_index_in_dim)/dynamic_slice | solution.py:223
  16.0 4.6 %copy.19 = bf16[4,1,256,512]{3,2,0,1:T(8,128)(2,1)S(1)} copy(bf16[4,1,256,512]{2,1,0,3:T(2,128)(2,1)} %get-tuple-element.6) | data formatting | bytes 2097152
  20.6 1.0 add.69
  21.6 1.6 %collective-permute-start.1 = (f32[4,128,128]{2,1,0:T(8,128)S(1)}, f32[4,128,128]{2,1,0:T(8,128)S(1)}, u32[]{:S(2)}, u32[]{:S(2)}) collective-permute-start(f32[4,128,128]{2,1,0:T(8,128)S(1)} %add.69), channel_id=1, source_target_pairs={{0,8},{8,0},{4,12},{12,4},{16,24},{24,16},{20,28},{28,20},{1,9},{9... | collective-permute-start | bytes 786440 | tf_op jit(solution)/shard_map/ppermute | solution.py:24
  23.2 0.8 dynamic-slice_convert_fusion
  24.1 0.5 collective-permute-start.3
  24.6 0.2 multiply_reduce_fusion.2
  24.8 0.8 iota_compare_fusion
  25.6 3.8 %collective-permute-done.1 = f32[4,128,128]{2,1,0:T(8,128)S(1)} collective-permute-done((f32[4,128,128]{2,1,0:T(8,128)S(1)}, f32[4,128,128]{2,1,0:T(8,128)S(1)}, u32[]{:S(2)}, u32[]{:S(2)}) %collective-permute-start.1) | collective-permute-done | bytes 262176 | tf_op jit(solution)/shard_map/ppermute | solution.py:24
  29.4 0.8 add.72
  30.2 2.6 %collective-permute-start.2 = (f32[4,128,128]{2,1,0:T(8,128)}, f32[4,128,128]{2,1,0:T(8,128)}, u32[]{:S(2)}, u32[]{:S(2)}) collective-permute-start(f32[4,128,128]{2,1,0:T(8,128)} %add.72), channel_id=1, source_target_pairs={{0,16},{16,0},{4,20},{20,4},{8,24},{24,8},{12,28},{28,12},{1,17},{... | collective-permute-start | bytes 786440 | tf_op jit(solution)/shard_map/ppermute | solution.py:24
  32.8 3.6 %fusion.1 = f32[4,128,512]{2,1,0:T(8,128)} fusion(bf16[512,4,128]{0,2,1:T(8,128)(2,1)S(1)} %bitcast.52, f32[4]{0:T(128)S(1)} %get-tuple-element.5, pred[512,512]{1,0:T(8,128)(4,1)} %iota_compare_fusion, bf16[512,512]{1,0:T(8,128)(2,1)} %param.7, bf16[512,512]{1,0:T(8,128)(2,1)S(1)} %copy-done), kind=kOutput, calls=%fused_computation.2 | convolution fusion | flops 540016640 | bytes 2883600 | tf_op jit(solution)/shard_map/chnm,cmhe->cnhe/dot_general | solution.py:279
  36.4 4.2 %copy.18 = bf16[4,1,256,512]{3,2,0,1:T(8,128)(2,1)} copy(bf16[4,1,256,512]{2,1,0,3:T(2,128)(2,1)S(1)} %copy-done.3) | data formatting | bytes 2097152
  40.7 1.6 %collective-permute-start.4 = (f32[1024,128]{1,0:T(8,128)}, f32[1024,128]{1,0:T(8,128)}, u32[]{:S(2)}, u32[]{:S(2)}) collective-permute-start(f32[1024,128]{1,0:T(8,128)} %collective-permute-done.3), channel_id=1, source_target_pairs={{0,2},{2,0},{1,3},{3,1},{4,6},{6,4},{5,7},{7,5},{8,10},{10,8},{9,1... | collective-permute-start | bytes 1572872 | tf_op jit(solution)/shard_map/ppermute | solution.py:24
  42.2 0.1 convolution_bitcast_fusion
  42.4 0.3 broadcast_in_dim.12
  42.6 1.1 constant_dynamic-update-slice_fusion.3
  43.8 0.3 collective-permute-done.2
  44.1 2.8 %fusion.3 = (f32[512]{0:T(512)S(1)}, f32[4,128,512]{2,1,0:T(8,128)}) fusion(f32[4,128,512]{2,1,0:T(8,128)S(1)} %copy-done.6, f32[4,128,128]{2,1,0:T(8,128)} %collective-permute-done.2, f32[4,128,128]{2,1,0:T(8,128)S(1)} %copy-done.5, f32[4,128,128]{2,1,0:T(8,128)} %collective-permute-done, f32[4,128,128]{2,1,0:T(8,128)S(1)} %fusion.5, ...), kind=kOutput, calls=%fused_computation.7 | convolution fusion | flops 404160000 | bytes 3672128 | tf_op jit(solution)/shard_map/cnhd,chde->cnhe/dot_general | solution.py:271
  46.9 9.1 %psum.7 = f32[512]{0:T(512)S(1)} all-reduce(f32[512]{0:T(512)S(1)} %get-tuple-element.8), channel_id=1, replica_groups=mesh['seq'=8,'head'=4] {'head'}, use_global_device_ids=true, to_apply=%region_1.2 | all-reduce | flops 512 | bytes 4096 | tf_op jit(solution)/shard_map/psum | solution.py:281
  56.0 0.1 collective-permute-start.6
  56.1 2.5 %copy.17 = f32[512,512]{1,0:T(8,128)} copy(f32[512,512]{0,1:T(8,128)} %bitcast.49) | data formatting | bytes 2097152 | tf_op jit(solution)/shard_map/reshape | solution.py:280
  58.6 1.4 %multiply_convert_fusion.normed_ref = bf16[512,512]{1,0:T(8,128)(2,1)S(1)} fusion(f32[512,512]{1,0:T(8,128)} %copy.17, f32[512]{0:T(512)S(1)} %add_rsqrt_fusion), kind=kLoop, calls=%fused_computation.8 | loop fusion | flops 524288 | bytes 1574912 | tf_op jit(solution)/shard_map/convert_element_type | solution.py:282
  60.1 1.3 %constant_dynamic-update-slice_fusion.2 = f32[1024,512]{1,0:T(8,128)S(1)} fusion(f32[1024,512]{1,0:T(8,128)S(1)} %constant_dynamic-update-slice_fusion.3, f32[1024,128]{1,0:T(8,128)} %collective-permute-done.4, s32[]{:T(128)S(6)} %select_n.52), kind=kLoop, calls=%fused_computation.38 | loop fusion | bytes 1048580 | tf_op jit(solution)/shard_map/dynamic_update_slice | solution.py:233
  61.4 1.1 constant_dynamic-update-slice_fusion.1
  62.5 0.1 constant_dynamic-update-slice_fusion.theirs_ref
  62.6 56.9 %shard_map.68 = f32[256,512]{1,0:T(8,128)S(1)} custom-call(bf16[1024,512]{1,0:T(8,128)(2,1)S(1)} %bitcast.48, f32[1024,512]{1,0:T(8,128)S(1)} %constant_dynamic-update-slice_fusion.theirs_ref, bf16[512,512]{1,0:T(8,128)(2,1)S(1)} %multiply_convert_fusion.normed_ref), custom_call_target="tpu_custom_call" | custom-call | tf_op jit(solution)/shard_map/pallas_call | solution.py:190
  119.5 0.8 copy.46
  (24 shorter events, 0.1 us)
Async XLA Ops:
  0.6 32.2 %copy-start = (bf16[512,512]{1,0:T(8,128)(2,1)S(1)}, bf16[512,512]{1,0:T(8,128)(2,1)}, u32[]{:S(2)}) copy-start(bf16[512,512]{1,0:T(8,128)(2,1)} %param.5) | copy-start | bytes 1572868
  3.3 17.3 %collective-permute-start = (f32[4,128,128]{2,1,0:T(8,128)S(1)}, f32[4,128,128]{2,1,0:T(8,128)}, u32[]{:S(2)}, u32[]{:S(2)}) collective-permute-start(f32[4,128,128]{2,1,0:T(8,128)S(1)} %fusion.5), channel_id=1, source_target_pairs={{0,4},{4,0},{8,12},{12,8},{16,20},{20,16},{24,28},{28,24},{1,5},{5... | collective-permute-start | bytes 786440 | tf_op jit(solution)/shard_map/ppermute | solution.py:24
  16.0 8.6 %copy-start.7 = (s32[4,20]{1,0:T(4,128)S(1)}, s32[4,20]{1,0:T(4,128)}, u32[]{:S(2)}) copy-start(s32[4,20]{1,0:T(4,128)} %param.8) | copy-start | bytes 964
  21.6 7.8 %collective-permute-start.1 = (f32[4,128,128]{2,1,0:T(8,128)S(1)}, f32[4,128,128]{2,1,0:T(8,128)S(1)}, u32[]{:S(2)}, u32[]{:S(2)}) collective-permute-start(f32[4,128,128]{2,1,0:T(8,128)S(1)} %add.69), channel_id=1, source_target_pairs={{0,8},{8,0},{4,12},{12,4},{16,24},{24,16},{20,28},{28,20},{1,9},{9... | collective-permute-start | bytes 786440 | tf_op jit(solution)/shard_map/ppermute | solution.py:24
  24.1 16.6 %collective-permute-start.3 = (f32[1024,128]{1,0:T(8,128)}, f32[1024,128]{1,0:T(8,128)}, u32[]{:S(2)}, u32[]{:S(2)}) collective-permute-start(f32[1024,128]{1,0:T(8,128)} %dynamic-slice_convert_fusion), channel_id=1, source_target_pairs={{0,4},{4,0},{8,12},{12,8},{16,20},{20,16},{24,28},{28,24},{1,5},{5... | collective-permute-start | bytes 1572872 | tf_op jit(solution)/shard_map/ppermute | solution.py:24
  29.4 3.4 %copy-start.4 = (f32[4,128,128]{2,1,0:T(8,128)}, f32[4,128,128]{2,1,0:T(8,128)S(1)}, u32[]{:S(2)}) copy-start(f32[4,128,128]{2,1,0:T(8,128)S(1)} %collective-permute-done.1) | copy-start | bytes 786436
  30.2 13.8 %collective-permute-start.2 = (f32[4,128,128]{2,1,0:T(8,128)}, f32[4,128,128]{2,1,0:T(8,128)}, u32[]{:S(2)}, u32[]{:S(2)}) collective-permute-start(f32[4,128,128]{2,1,0:T(8,128)} %add.72), channel_id=1, source_target_pairs={{0,16},{16,0},{4,20},{20,4},{8,24},{24,8},{12,28},{28,12},{1,17},{... | collective-permute-start | bytes 786440 | tf_op jit(solution)/shard_map/ppermute | solution.py:24
  32.8 3.6 %copy-start.3 = (bf16[4,1,256,512]{2,1,0,3:T(2,128)(2,1)S(1)}, bf16[4,1,256,512]{2,1,0,3:T(2,128)(2,1)}, u32[]{:S(2)}) copy-start(bf16[4,1,256,512]{2,1,0,3:T(2,128)(2,1)} %get-tuple-element.7) | copy-start | bytes 3145732
  40.7 3.4 %copy-start.5 = (f32[4,128,128]{2,1,0:T(8,128)S(1)}, f32[4,128,128]{2,1,0:T(8,128)}, u32[]{:S(2)}) copy-start(f32[4,128,128]{2,1,0:T(8,128)} %copy-done.4) | copy-start | bytes 786436
  40.7 3.4 %copy-start.6 = (f32[4,128,512]{2,1,0:T(8,128)S(1)}, f32[4,128,512]{2,1,0:T(8,128)}, u32[]{:S(2)}) copy-start(f32[4,128,512]{2,1,0:T(8,128)} %fusion.1) | copy-start | bytes 3145732
  40.7 15.3 %collective-permute-start.4 = (f32[1024,128]{1,0:T(8,128)}, f32[1024,128]{1,0:T(8,128)}, u32[]{:S(2)}, u32[]{:S(2)}) collective-permute-start(f32[1024,128]{1,0:T(8,128)} %collective-permute-done.3), channel_id=1, source_target_pairs={{0,2},{2,0},{1,3},{3,1},{4,6},{6,4},{5,7},{7,5},{8,10},{10,8},{9,1... | collective-permute-start | bytes 1572872 | tf_op jit(solution)/shard_map/ppermute | solution.py:24
  42.4 19.0 %collective-permute-start.5 = (f32[1024,128]{1,0:T(8,128)}, f32[1024,128]{1,0:T(8,128)}, u32[]{:S(2)}, u32[]{:S(2)}) collective-permute-start(f32[1024,128]{1,0:T(8,128)} %collective-permute-done.3), channel_id=1, source_target_pairs={{0,1},{1,0},{2,3},{3,2},{4,5},{5,4},{6,7},{7,6},{8,9},{9,8},{10,11... | collective-permute-start | bytes 1572872 | tf_op jit(solution)/shard_map/ppermute | solution.py:24
  56.0 6.5 %collective-permute-start.6 = (f32[1024,128]{1,0:T(8,128)}, f32[1024,128]{1,0:T(8,128)S(1)}, u32[]{:S(2)}, u32[]{:S(2)}) collective-permute-start(f32[1024,128]{1,0:T(8,128)} %collective-permute-done.4), channel_id=1, source_target_pairs={{0,1},{1,0},{2,3},{3,2},{4,5},{5,4},{6,7},{7,6},{8,9},{9,8},{10,11... | collective-permute-start | bytes 1572872 | tf_op jit(solution)/shard_map/ppermute | solution.py:24
  58.6 4.0 %copy-start.1 = (bf16[4,1,256,512]{3,2,0,1:T(8,128)(2,1)S(1)}, bf16[4,1,256,512]{3,2,0,1:T(8,128)(2,1)}, u32[]{:S(2)}) copy-start(bf16[4,1,256,512]{3,2,0,1:T(8,128)(2,1)} %copy.18) | copy-start | bytes 3145732
  60.1 59.5 %copy-start.2 = (bf16[512,512]{1,0:T(8,128)(2,1)}, bf16[512,512]{1,0:T(8,128)(2,1)S(1)}, u32[]{:S(2)}) copy-start(bf16[512,512]{1,0:T(8,128)(2,1)S(1)} %multiply_convert_fusion.normed_ref) | copy-start | bytes 1572868

commit v2 on v0

v2 whole, which is shorter than its diff:
```python
import functools

import jax
import jax.numpy as jnp
from jax import lax
from jax.experimental import pallas as pl
from jax.experimental.pallas import tpu as pltpu
from jax.sharding import PartitionSpec as P

D = 2048
HEADS = 16
GROUP = 512
MESH = pl.DeviceIdType.MESH
NT = (((1,), (1,)), ((), ()))
TN = (((0,), (0,)), ((), ()))


def flip(index, mask):
    bit = 1
    while bit <= mask:
        if mask & bit:
            index = index + bit - 2 * bit * ((index // bit) % 2)
        bit *= 2
    return index


def matmul(a, b, dims=(((1,), (0,)), ((), ()))):
    return lax.dot_general(a, b, dims, preferred_element_type=jnp.float32)


def split(x):
    high = x.astype(jnp.bfloat16)
    return high, (x - high.astype(jnp.float32)).astype(jnp.bfloat16)


def kernel(
    line,
    heads,
    q_ref,
    k_ref,
    v_ref,
    level_ref,
    grad_ref,
    normed_ref,
    out_ref,
    state,
    pair_state,
    block,
    line_state,
    give,
    mix,
    turned,
    quarter,
    theirs,
    theirs_half,
    raw,
    came,
    squares,
    squares_in,
    root,
    root_in,
    part,
    rising,
    falling,
    state_send,
    state_recv,
    grad_send,
    grad_recv,
    square_send,
    square_recv,
    root_send,
    root_recv,
    pair_send,
    pair_recv,
    up_send,
    up_recv,
    down_send,
    down_recv,
):
    me = lax.axis_index("seq")
    head = lax.axis_index("head")
    place = me // 2
    side = me % 2
    other = flip(me, 1)
    above = me + 2
    below = me - 2
    tokens, width = q_ref.shape
    lanes = D // HEADS
    chunks = width // lanes
    half = chunks // 2
    rows = out_ref.shape[0]
    line_bits = line.bit_length() - 1
    head_bits = heads.bit_length() - 1
    share = line // heads
    scale = lanes ** (-0.5)
    low_end = place == 0
    high_end = place == line - 1
    inner = jnp.logical_and(place > 0, place < line - 1)

    def span(k):
        return slice(k * lanes, (k + 1) * lanes)

    barrier = pltpu.get_barrier_semaphore()

    def greet(device):
        pl.semaphore_signal(barrier, inc=1, device_id=device, device_id_type=MESH)

    greet({"seq": other})
    for b in range(line_bits):
        greet({"seq": flip(me, 2 << b)})
    for r in range(1, heads):
        greet({"head": flip(head, r)})

    @pl.when(place < line - 1)
    def _():
        greet({"seq": above})

    @pl.when(place > 0)
    def _():
        greet({"seq": below})

    def remote(src, dst, send, recv, device):
        return pltpu.make_async_remote_copy(
            src_ref=src,
            dst_ref=dst,
            send_sem=send,
            recv_sem=recv,
            device_id=device,
            device_id_type=MESH,
        )

    def state_copy():
        return remote(
            state.at[pl.ds((1 - side) * half, half)],
            pair_state,
            state_send.at[0],
            state_recv.at[0],
            {"seq": other},
        )

    def line_copy(b):
        return remote(
            block.at[b],
            line_state.at[b],
            state_send.at[1 + b],
            state_recv.at[1 + b],
            {"seq": flip(me, 2 << b)},
        )

    def give_copy():
        return remote(
            give,
            mix.at[pl.ds(side * half, half)],
            state_send.at[1 + line_bits],
            state_recv.at[1 + line_bits],
            {"seq": other},
        )

    def grad_copy():
        return remote(
            quarter,
            theirs.at[pl.ds(head * share, share)],
            grad_send.at[0],
            grad_recv.at[0],
            {"seq": other},
        )

    def share_copy(r, bit):
        owned = theirs.at[pl.ds(flip(head, r) * share, share)]
        slot = r ^ (1 << bit)
        return remote(
            owned, owned, grad_send.at[slot], grad_recv.at[slot], {"head": flip(head, 1 << bit)}
        )

    def square_copy(r):
        return remote(
            squares,
            squares_in.at[r - 1],
            square_send.at[r - 1],
            square_recv.at[r - 1],
            {"head": flip(head, r)},
        )

    def root_copy():
        return remote(root, root_in, root_send.at[0], root_recv.at[0], {"seq": other})

    def pair_copy(k):
        return remote(raw.at[k], came.at[k], pair_send.at[k], pair_recv.at[k], {"seq": other})

    def up_copy(k, d):
        return remote(
            part.at[k, d], rising.at[k, d], up_send.at[k, d], up_recv.at[k, d], {"seq": above}
        )

    def down_copy(k, d):
        return remote(
            part.at[k, d], falling.at[k, d], down_send.at[k, d], down_recv.at[k, d], {"seq": below}
        )

    for h in range(chunks):
        state[h] = matmul(k_ref[:, span(h)], v_ref[:, span(h)], TN)
    peers = line_bits + heads + jnp.where(place > 0, 1, 0) + jnp.where(place < line - 1, 1, 0)
    pl.semaphore_wait(barrier, peers)
    state_copy().start()

    tile = max(rows, lanes)
    for j in range(grad_ref.shape[1] // tile):
        flat = grad_ref[:, j * tile : (j + 1) * tile].T
        for i in range(tile // rows):
            owner = j * (tile // rows) + i
            turned[owner % 2, owner // 2] = flat[i * rows : (i + 1) * rows]
    quarter[...] = turned[1 - side, pl.ds(head * share, share)].astype(jnp.float32)
    grad_copy().start()

    def near(h):
        weight = scale * level_ref[h, 0].astype(jnp.float32)
        scores = matmul(q_ref[:, span(h)], k_ref[:, span(h)], NT) * weight
        row = lax.broadcasted_iota(jnp.int32, scores.shape, 0)
        column = lax.broadcasted_iota(jnp.int32, scores.shape, 1)
        probs = jnp.where(column <= row, scores, 0.0).astype(jnp.bfloat16)
        raw[h] = matmul(probs, v_ref[:, span(h)])

    def level(i, number):
        return level_ref[side * half + i, number].astype(jnp.float32)

    own = pl.ds(side * half, half)
    state_copy().wait_recv()
    block[0] = state[own] + pair_state[...]
    done = 0
    for b in range(line_bits):
        upper = (place // (1 << b)) % 2
        last = b == line_bits - 1
        if last:

            @pl.when(upper == 0)
            def _():
                line_copy(b).start()
        else:
            line_copy(b).start()
        until = chunks * (b + 1) // line_bits
        for h in range(done, until):
            near(h)
        done = until
        if last:

            @pl.when(upper == 1)
            def _():
                line_copy(b).wait_recv()

            @pl.when(upper == 0)
            def _():
                line_state[b] = jnp.zeros(line_state.shape[1:], jnp.float32)
        else:
            line_copy(b).wait_recv()
            block[b + 1] = block[b] + line_state[b]
    for i in range(half):
        far = jnp.zeros((lanes, lanes), jnp.float32)
        for b in range(line_bits):
            upper = ((place // (1 << b)) % 2).astype(jnp.float32)
            far = far + (level(i, 2 + b) * upper) * line_state[b, i]
        first = level(i, 1)
        right = side.astype(jnp.float32)
        mix[side * half + i] = far + (first * right) * pair_state[i]
        give[i] = far + (first * (1.0 - right)) * state[side * half + i]
    give_copy().start()

    owned = [0]
    stages = list(reversed(range(head_bits)))
    grad_copy().wait_recv()

    def forward(bit):
        for r in owned:
            share_copy(r, bit).start()

    def collect(bit):
        for r in list(owned):
            share_copy(r, bit).wait_recv()
            owned.append(r ^ (1 << bit))

    forward(stages[0])
    give_copy().wait_recv()

    total = jnp.zeros((tokens, lanes), jnp.float32)
    for h in range(chunks):
        high, low = split(mix[h])
        query = q_ref[:, span(h)]
        value = raw[h] + scale * (matmul(query, high) + matmul(query, low))
        raw[h] = value
        pair_copy(h).start()
        total = total + value * value
    ones = jnp.ones((8, lanes), jnp.bfloat16)
    high, low = split(total)
    squares[...] = matmul(ones, high, NT) + matmul(ones, low, NT)
    for r in range(1, heads):
        square_copy(r).start()
    collect(stages[0])
    for r in range(1, heads):
        square_copy(r).wait_recv()
    whole = squares[...]
    for r in range(1, heads):
        whole = whole + squares_in[r - 1]
    root[...] = lax.rsqrt(whole / D + 1e-06)
    root_copy().start()
    for bit in stages[1:]:
        forward(bit)
        if bit != stages[-1]:
            collect(bit)
    inverse = root[...].T[:, :1]
    for h in range(chunks):
        normed_ref[:, span(h)] = (raw[h] * inverse).astype(jnp.bfloat16)
    root_copy().wait_recv()
    their_inverse = root_in[...].T[:, :1]
    if len(stages) > 1:
        collect(stages[-1])
    theirs_half[...] = theirs[...].reshape(theirs_half.shape).astype(jnp.bfloat16)

    def ends(k):
        @pl.when(low_end)
        def _():
            @pl.loop(0, line - 1)
            def _(i):
                up_copy(k, line - 1 - i).start()

        @pl.when(high_end)
        def _():
            @pl.loop(0, line - 1)
            def _(d):
                down_copy(k, d).start()

    def middle(k):
        @pl.when(inner)
        def _():
            @pl.loop(0, line - 1 - place)
            def _(i):
                d = line - 1 - i
                up_copy(k, d).wait_recv()
                part[k, d] = part[k, d] + rising[k, d]
                up_copy(k, d).start()

            @pl.loop(0, place)
            def _(d):
                down_copy(k, d).wait_recv()
                part[k, d] = part[k, d] + falling[k, d]
                down_copy(k, d).start()

    for k in range(chunks):
        mine = turned[side].reshape(line * rows, tokens)
        product = matmul(mine, normed_ref[:, span(k)])
        pair_copy(k).wait_recv()
        there = (came[k] * their_inverse).astype(jnp.bfloat16)
        product = product + matmul(theirs_half[...], there)
        part[k] = product.reshape(part.shape[1:])
        ends(k)
        if k:
            middle(k - 1)
    middle(chunks - 1)

    for k in range(chunks):
        out_ref[:, span(k)] = part[k, place]

        @pl.when(place > 0)
        def _():
            up_copy(k, place).wait_recv()
            out_ref[:, span(k)] = out_ref[:, span(k)] + rising[k, place]

        @pl.when(place < line - 1)
        def _():
            down_copy(k, place).wait_recv()
            out_ref[:, span(k)] = out_ref[:, span(k)] + falling[k, place]

    state_copy().wait_send()
    for b in range(line_bits - 1):
        line_copy(b).wait_send()

    @pl.when((place // (line // 2)) % 2 == 0)
    def _():
        line_copy(line_bits - 1).wait_send()

    give_copy().wait_send()
    grad_copy().wait_send()
    held = [0]
    for bit in stages:
        for r in list(held):
            share_copy(r, bit).wait_send()
            held.append(r ^ (1 << bit))
    for r in range(1, heads):
        square_copy(r).wait_send()
    root_copy().wait_send()
    for k in range(chunks):
        pair_copy(k).wait_send()

        @pl.loop(place + 1, line)
        def _(d):
            up_copy(k, d).wait_send()

        @pl.loop(0, place)
        def _(d):
            down_copy(k, d).wait_send()


def body(queries, keys, values, level_weights, out_grad):
    tokens, width = queries.shape
    assert tokens == GROUP
    count = lax.axis_size("seq")
    heads = lax.axis_size("head")
    line = count // 2
    line_bits = line.bit_length() - 1
    lanes = D // HEADS
    chunks = width // lanes
    half = chunks // 2
    rows = out_grad.shape[1] // count
    slots = (chunks, line, rows, lanes)
    states = (half, lanes, lanes)
    vmem = pl.BlockSpec(memory_space=pltpu.VMEM)
    smem = pl.BlockSpec(memory_space=pltpu.SMEM)
    f32 = jnp.float32
    dma = pltpu.SemaphoreType.DMA
    return pl.pallas_call(
        functools.partial(kernel, line, heads),
        out_shape=(
            jax.ShapeDtypeStruct((tokens, width), jnp.bfloat16),
            jax.ShapeDtypeStruct((rows, width), f32),
        ),
        in_specs=[vmem, vmem, vmem, smem, vmem],
        out_specs=(vmem, vmem),
        scratch_shapes=[
            pltpu.VMEM((chunks, lanes, lanes), f32),
            pltpu.VMEM(states, f32),
            pltpu.VMEM((line_bits, *states), f32),
            pltpu.VMEM((line_bits, *states), f32),
            pltpu.VMEM(states, f32),
            pltpu.VMEM((chunks, lanes, lanes), f32),
            pltpu.VMEM((2, line, rows, tokens), jnp.bfloat16),
            pltpu.VMEM((line // heads, rows, tokens), f32),
            pltpu.VMEM((line, rows, tokens), f32),
            pltpu.VMEM((line * rows, tokens), jnp.bfloat16),
            pltpu.VMEM((chunks, tokens, lanes), f32),
            pltpu.VMEM((chunks, tokens, lanes), f32),
            pltpu.VMEM((8, tokens), f32),
            pltpu.VMEM((heads - 1, 8, tokens), f32),
            pltpu.VMEM((8, tokens), f32),
            pltpu.VMEM((8, tokens), f32),
            pltpu.VMEM(slots, f32),
            pltpu.VMEM(slots, f32),
            pltpu.VMEM(slots, f32),
            dma((2 + line_bits,)),
            dma((2 + line_bits,)),
            dma((heads,)),
            dma((heads,)),
            dma((heads - 1,)),
            dma((heads - 1,)),
            dma((1,)),
            dma((1,)),
            dma((chunks,)),
            dma((chunks,)),
            dma((chunks, line)),
            dma((chunks, line)),
            dma((chunks, line)),
            dma((chunks, line)),
        ],
        compiler_params=pltpu.CompilerParams(
            collective_id=0, has_side_effects=True, vmem_limit_bytes=48 << 20
        ),
    )(queries, keys, values, level_weights, out_grad)


def solution(mesh):
    return jax.shard_map(
        body,
        mesh=mesh,
        in_specs=(
            P("seq", "head"),
            P("seq", "head"),
            P("seq", "head"),
            P("head", None),
            P("seq", None),
        ),
        out_specs=(P("seq", "head"), P("seq", "head")),
        check_vma=False,
    )
```

time: 157 us -> 101 us (0.64)
  waiting for transfers between devices: 107 us -> 0 us
  Pallas kernels: 0 us -> 93.4 us
  between operations: 14.1 us -> 0.65 us
  matrix products: 12.2 us -> 0 us
  starting transfers between devices: 7.43 us -> 0 us
  blocking collectives: 5.63 us -> 0 us
  other arithmetic: 4.25 us -> 0 us
    pallas_call x0 -> x1, Pallas kernels: none -> 93.4 us  [body(): pl.pallas_call(functools.partial(kernel, line, heads), out_shape=(jax.Sha...]
    reduce_scatter x1 -> x0, waiting for transfers between devices: 90 us -> none  [body(): lax.psum_scatter(whole_term, 'seq', scatter_dimension=0, tiled=True)]
    ppermute x3 -> x0, waiting for transfers between devices: 17 us -> none  [partner_2(): return lax.ppermute(block, axis, route)]
    dot_general x5 -> x0, matrix products: 12.2 us -> none  [the longest x1 3.61 us: body(): jnp.einsum('chnm,cmhe->cnhe', probs, v_blocks, preferred_element_type=jnp...]
    ppermute x3 -> x0, starting transfers between devices: 7.39 us -> none  [partner_2(): return lax.ppermute(block, axis, route)]
    psum x1 -> x0, blocking collectives: 5.63 us -> none  [body(): row_squares = lax.psum(jnp.sum(raw * raw, axis=1), 'head')]
    unnamed x5 -> x12, local copies, waits for them, and re-layouts: 2.83 us -> 6.98 us
    add x2 -> x0, other arithmetic: 2.41 us -> none  [body(): block = block + partner]
  transfers between devices with their start and end apart: 4 -> 0, of which waited for: 4 -> 0; matrix products, arithmetic and copies ran while one was open for 4% -> 0% of each run, Pallas kernels for 0% -> 0%
where the time goes in v2:
time: 101 us
  Pallas kernels  93.4 us (92%)
  local copies, waits for them, and re-layouts  6.98 us (7%)
    pallas_call x1, Pallas kernels, body(): pl.pallas_call(functools.partial(kernel, line, heads), out_shape=(jax.Sha...  93.4 us
    unnamed x12, local copies, waits for them, and re-layouts  6.98 us

profile of v2, /device:TPU:0, one launch (start us, length us, event | category | flops | bytes accessed | tf_op | source)
XLA Modules:
  0.0 101.0 jit_solution(15108243865343013318)
XLA Ops:
  0.6 0.0 copy-start
  0.6 1.6 %copy-done = bf16[512,2048]{1,0:T(8,128)(2,1)S(1)} copy-done((bf16[512,2048]{1,0:T(8,128)(2,1)S(1)}, bf16[512,2048]{1,0:T(8,128)(2,1)}, u32[]{:S(2)}) %copy-start) | copy-done | bytes 2097176
  2.2 0.0 copy-start.1
  2.2 1.0 %copy-done.1 = bf16[512,512]{1,0:T(8,128)(2,1)S(1)} copy-done((bf16[512,512]{1,0:T(8,128)(2,1)S(1)}, bf16[512,512]{1,0:T(8,128)(2,1)}, u32[]{:S(2)}) %copy-start.1) | copy-done | bytes 524312
  3.3 0.0 copy-start.2
  3.3 1.0 %copy-done.2 = bf16[512,512]{1,0:T(8,128)(2,1)S(1)} copy-done((bf16[512,512]{1,0:T(8,128)(2,1)S(1)}, bf16[512,512]{1,0:T(8,128)(2,1)}, u32[]{:S(2)}) %copy-start.2) | copy-done | bytes 524312
  4.3 0.0 copy-start.3
  4.3 1.0 %copy-done.3 = bf16[512,512]{1,0:T(8,128)(2,1)S(1)} copy-done((bf16[512,512]{1,0:T(8,128)(2,1)S(1)}, bf16[512,512]{1,0:T(8,128)(2,1)}, u32[]{:S(2)}) %copy-start.3) | copy-done | bytes 524312
  5.3 0.0 copy-start.4
  5.4 0.7 copy-done.4
  6.0 93.4 %shard_map.68 = (bf16[512,512]{1,0:T(8,128)(2,1)S(1)}, f32[256,512]{1,0:T(8,128)S(1)}) custom-call(bf16[512,512]{1,0:T(8,128)(2,1)S(1)} %copy-done.1, bf16[512,512]{1,0:T(8,128)(2,1)S(1)} %copy-done.2, bf16[512,512]{1,0:T(8,128)(2,1)S(1)} %copy-done.3, s32[4,20]{1,0:T(4,128)S(1)} %copy-done.4, bf16[512,2048]{1,0:T(8,128)(2,1)S(1)} %copy-done), custom_call_target="tpu_custom_call" | custom-call | tf_op jit(solution)/shard_map/pallas_call | solution.py:418
  99.4 0.8 copy.9
  100.2 0.8 copy.10
Async XLA Ops:
  0.6 1.6 %copy-start = (bf16[512,2048]{1,0:T(8,128)(2,1)S(1)}, bf16[512,2048]{1,0:T(8,128)(2,1)}, u32[]{:S(2)}) copy-start(bf16[512,2048]{1,0:T(8,128)(2,1)} %grad_ref.1) | copy-start | bytes 6291460
  2.2 1.0 %copy-start.1 = (bf16[512,512]{1,0:T(8,128)(2,1)S(1)}, bf16[512,512]{1,0:T(8,128)(2,1)}, u32[]{:S(2)}) copy-start(bf16[512,512]{1,0:T(8,128)(2,1)} %q_ref.1) | copy-start | bytes 1572868
  3.3 1.0 %copy-start.2 = (bf16[512,512]{1,0:T(8,128)(2,1)S(1)}, bf16[512,512]{1,0:T(8,128)(2,1)}, u32[]{:S(2)}) copy-start(bf16[512,512]{1,0:T(8,128)(2,1)} %k_ref.1) | copy-start | bytes 1572868
  4.3 1.0 %copy-start.3 = (bf16[512,512]{1,0:T(8,128)(2,1)S(1)}, bf16[512,512]{1,0:T(8,128)(2,1)}, u32[]{:S(2)}) copy-start(bf16[512,512]{1,0:T(8,128)(2,1)} %v_ref.1) | copy-start | bytes 1572868
  5.3 0.7 copy-start.4

commit v3 on v2

--- a/solution.py
+++ b/solution.py
@@ -36,13 +36,18 @@
 def kernel(
     line,
     heads,
+    q_in,
+    k_in,
+    v_in,
+    level_ref,
+    grad_in,
+    normed_ref,
+    out_ref,
     q_ref,
     k_ref,
     v_ref,
-    level_ref,
     grad_ref,
-    normed_ref,
-    out_ref,
+    loads,
     state,
     pair_state,
     block,
@@ -95,10 +100,14 @@
     scale = lanes ** (-0.5)
     low_end = place == 0
     high_end = place == line - 1
-    inner = jnp.logical_and(place > 0, place < line - 1)
 
     def span(k):
         return slice(k * lanes, (k + 1) * lanes)
+
+    pairs = ((k_in, k_ref), (v_in, v_ref), (grad_in, grad_ref), (q_in, q_ref))
+    copies = [pltpu.make_async_copy(a, b, loads.at[i]) for i, (a, b) in enumerate(pairs)]
+    for copy in copies:
+        copy.start()
 
     barrier = pltpu.get_barrier_semaphore()
 
@@ -197,12 +206,15 @@
             part.at[k, d], falling.at[k, d], down_send.at[k, d], down_recv.at[k, d], {"seq": below}
         )
 
+    copies[0].wait()
+    copies[1].wait()
     for h in range(chunks):
         state[h] = matmul(k_ref[:, span(h)], v_ref[:, span(h)], TN)
     peers = line_bits + heads + jnp.where(place > 0, 1, 0) + jnp.where(place < line - 1, 1, 0)
     pl.semaphore_wait(barrier, peers)
     state_copy().start()
 
+    copies[2].wait()
     tile = max(rows, lanes)
     for j in range(grad_ref.shape[1] // tile):
         flat = grad_ref[:, j * tile : (j + 1) * tile].T
@@ -223,6 +235,7 @@
     def level(i, number):
         return level_ref[side * half + i, number].astype(jnp.float32)
 
+    copies[3].wait()
     own = pl.ds(side * half, half)
     state_copy().wait_recv()
     block[0] = state[own] + pair_state[...]
@@ -327,21 +340,31 @@
             def _(d):
                 down_copy(k, d).start()
 
+    def rise(k):
+        @pl.loop(0, line - 1 - place)
+        def _(i):
+            d = line - 1 - i
+            up_copy(k, d).wait_recv()
+            part[k, d] = part[k, d] + rising[k, d]
+            up_copy(k, d).start()
+
+    def fall(k):
+        @pl.loop(0, place)
+        def _(d):
+            down_copy(k, d).wait_recv()
+            part[k, d] = part[k, d] + falling[k, d]
+            down_copy(k, d).start()
+
     def middle(k):
-        @pl.when(inner)
+        @pl.when(jnp.logical_and(place > 0, place < line // 2))
         def _():
-            @pl.loop(0, line - 1 - place)
-            def _(i):
-                d = line - 1 - i
-                up_copy(k, d).wait_recv()
-                part[k, d] = part[k, d] + rising[k, d]
-                up_copy(k, d).start()
-
-            @pl.loop(0, place)
-            def _(d):
-                down_copy(k, d).wait_recv()
-                part[k, d] = part[k, d] + falling[k, d]
-                down_copy(k, d).start()
+            rise(k)
+            fall(k)
+
+        @pl.when(jnp.logical_and(place >= line // 2, place < line - 1))
+        def _():
+            fall(k)
+            rise(k)
 
     for k in range(chunks):
         mine = turned[side].reshape(line * rows, tokens)
@@ -413,6 +436,7 @@
     states = (half, lanes, lanes)
     vmem = pl.BlockSpec(memory_space=pltpu.VMEM)
     smem = pl.BlockSpec(memory_space=pltpu.SMEM)
+    away = pl.BlockSpec(memory_space=pl.ANY)
     f32 = jnp.float32
     dma = pltpu.SemaphoreType.DMA
     return pl.pallas_call(
@@ -421,9 +445,14 @@
             jax.ShapeDtypeStruct((tokens, width), jnp.bfloat16),
             jax.ShapeDtypeStruct((rows, width), f32),
         ),
-        in_specs=[vmem, vmem, vmem, smem, vmem],
+        in_specs=[away, away, away, smem, away],
         out_specs=(vmem, vmem),
         scratch_shapes=[
+            pltpu.VMEM(queries.shape, queries.dtype),
+            pltpu.VMEM(keys.shape, keys.dtype),
+            pltpu.VMEM(values.shape, values.dtype),
+            pltpu.VMEM(out_grad.shape, out_grad.dtype),
+            pltpu.SemaphoreType.DMA((4,)),
             pltpu.VMEM((chunks, lanes, lanes), f32),
             pltpu.VMEM(states, f32),
             pltpu.VMEM((line_bits, *states), f32),
@@ -459,7 +488,7 @@
             dma((chunks, line)),
         ],
         compiler_params=pltpu.CompilerParams(
-            collective_id=0, has_side_effects=True, vmem_limit_bytes=48 << 20
+            collective_id=0, has_side_effects=True, vmem_limit_bytes=60 << 20
         ),
     )(queries, keys, values, level_weights, out_grad)
 

time: 101 us -> 93.9 us (0.930)
  Pallas kernels: 93.4 us -> 89.3 us
  local copies, waits for them, and re-layouts: 6.98 us -> 3.74 us
    pallas_call x1, Pallas kernels: 93.4 us -> 89.3 us  [body(): pl.pallas_call(functools.partial(kernel, line, heads), out_shape=(jax.Sha...]
    unnamed x12 -> x2, local copies, waits for them, and re-layouts: 6.98 us -> 3.74 us
where the time goes in v3:
time: 93.9 us; the launch traced here: 93.7 us
  Pallas kernels  89.3 us (95%)
  local copies, waits for them, and re-layouts  3.74 us (4%)
    pallas_call x1, Pallas kernels, body(): pl.pallas_call(functools.partial(kernel, line, heads), out_shape=(jax.Sha...  89.3 us
    unnamed x2, local copies, waits for them, and re-layouts  3.74 us

profile of v3, /device:TPU:0, one launch (start us, length us, event | category | flops | bytes accessed | tf_op | source)
XLA Modules:
  0.0 93.7 jit_solution(4048105275403428790)
XLA Ops:
  0.6 89.3 %shard_map.68 = (bf16[512,512]{1,0:T(8,128)(2,1)}, f32[256,512]{1,0:T(8,128)}) custom-call(bf16[512,512]{1,0:T(8,128)(2,1)} %q_in.1, bf16[512,512]{1,0:T(8,128)(2,1)} %k_in.1, bf16[512,512]{1,0:T(8,128)(2,1)} %v_in.1, s32[4,20]{1,0:T(4,128)} %level_ref.1, bf16[512,2048]{1,0:T(8,128)(2,1)} %grad_in.1), custom_call_target="tpu_custom_call" | custom-call | tf_op jit(solution)/shard_map/pallas_call | solution.py:442
  90.0 1.9 %copy.9 = bf16[512,512]{1,0:T(8,128)(2,1)} copy(bf16[512,512]{1,0:T(8,128)(2,1)} %get-tuple-element.4) | data formatting | bytes 1048576
  91.8 1.9 %copy.10 = f32[256,512]{1,0:T(8,128)} copy(f32[256,512]{1,0:T(8,128)} %get-tuple-element.5) | data formatting | bytes 1048576

commit v4 on v3

--- a/solution.py
+++ b/solution.py
@@ -10,6 +10,7 @@
 D = 2048
 HEADS = 16
 GROUP = 512
+PIECES = 2
 MESH = pl.DeviceIdType.MESH
 NT = (((1,), (1,)), ((), ()))
 TN = (((0,), (0,)), ((), ()))
@@ -97,6 +98,11 @@
     line_bits = line.bit_length() - 1
     head_bits = heads.bit_length() - 1
     share = line // heads
+    piece = rows // PIECES
+    stages = list(reversed(range(head_bits)))
+    held = [[0]]
+    for bit in stages:
+        held.append(held[-1] + [r ^ (1 << bit) for r in held[-1]])
     scale = lanes ** (-0.5)
     low_end = place == 0
     high_end = place == line - 1
@@ -165,20 +171,24 @@
             {"seq": other},
         )
 
-    def grad_copy():
-        return remote(
-            quarter,
-            theirs.at[pl.ds(head * share, share)],
-            grad_send.at[0],
-            grad_recv.at[0],
+    def grad_copy(p):
+        return remote(
+            quarter.at[:, pl.ds(p * piece, piece)],
+            theirs.at[pl.ds(head * share, share), pl.ds(p * piece, piece)],
+            grad_send.at[0, p],
+            grad_recv.at[0, p],
             {"seq": other},
         )
 
-    def share_copy(r, bit):
-        owned = theirs.at[pl.ds(flip(head, r) * share, share)]
+    def share_copy(r, bit, p):
+        owned = theirs.at[pl.ds(flip(head, r) * share, share), pl.ds(p * piece, piece)]
         slot = r ^ (1 << bit)
         return remote(
-            owned, owned, grad_send.at[slot], grad_recv.at[slot], {"head": flip(head, 1 << bit)}
+            owned,
+            owned,
+            grad_send.at[slot, p],
+            grad_recv.at[slot, p],
+            {"head": flip(head, 1 << bit)},
         )
 
     def square_copy(r):
@@ -222,7 +232,16 @@
             owner = j * (tile // rows) + i
             turned[owner % 2, owner // 2] = flat[i * rows : (i + 1) * rows]
     quarter[...] = turned[1 - side, pl.ds(head * share, share)].astype(jnp.float32)
-    grad_copy().start()
+    for p in range(PIECES):
+        grad_copy(p).start()
+
+    def forward(i, p):
+        for r in held[i]:
+            share_copy(r, stages[i], p).start()
+
+    def collect(i, p):
+        for r in held[i]:
+            share_copy(r, stages[i], p).wait_recv()
 
     def near(h):
         weight = scale * level_ref[h, 0].astype(jnp.float32)
@@ -255,6 +274,8 @@
             near(h)
         done = until
         if last:
+            grad_copy(0).wait_recv()
+            forward(0, 0)
 
             @pl.when(upper == 1)
             def _():
@@ -277,20 +298,9 @@
         give[i] = far + (first * (1.0 - right)) * state[side * half + i]
     give_copy().start()
 
-    owned = [0]
-    stages = list(reversed(range(head_bits)))
-    grad_copy().wait_recv()
-
-    def forward(bit):
-        for r in owned:
-            share_copy(r, bit).start()
-
-    def collect(bit):
-        for r in list(owned):
-            share_copy(r, bit).wait_recv()
-            owned.append(r ^ (1 << bit))
-
-    forward(stages[0])
+    for p in range(1, PIECES):
+        grad_copy(p).wait_recv()
+        forward(0, p)
     give_copy().wait_recv()
 
     total = jnp.zeros((tokens, lanes), jnp.float32)
@@ -306,7 +316,8 @@
     squares[...] = matmul(ones, high, NT) + matmul(ones, low, NT)
     for r in range(1, heads):
         square_copy(r).start()
-    collect(stages[0])
+    collect(0, 0)
+    forward(1, 0)
     for r in range(1, heads):
         square_copy(r).wait_recv()
     whole = squares[...]
@@ -314,17 +325,19 @@
         whole = whole + squares_in[r - 1]
     root[...] = lax.rsqrt(whole / D + 1e-06)
     root_copy().start()
-    for bit in stages[1:]:
-        forward(bit)
-        if bit != stages[-1]:
-            collect(bit)
+    for p in range(1, PIECES):
+        collect(0, p)
+        forward(1, p)
     inverse = root[...].T[:, :1]
     for h in range(chunks):
         normed_ref[:, span(h)] = (raw[h] * inverse).astype(jnp.bfloat16)
     root_copy().wait_recv()
     their_inverse = root_in[...].T[:, :1]
-    if len(stages) > 1:
-        collect(stages[-1])
+    for i in range(1, head_bits):
+        for p in range(PIECES):
+            if i > 1:
+                forward(i, p)
+            collect(i, p)
     theirs_half[...] = theirs[...].reshape(theirs_half.shape).astype(jnp.bfloat16)
 
     def ends(k):
@@ -400,12 +413,11 @@
         line_copy(line_bits - 1).wait_send()
 
     give_copy().wait_send()
-    grad_copy().wait_send()
-    held = [0]
-    for bit in stages:
-        for r in list(held):
-            share_copy(r, bit).wait_send()
-            held.append(r ^ (1 << bit))
+    for p in range(PIECES):
+        grad_copy(p).wait_send()
+        for i in range(head_bits):
+            for r in held[i]:
+                share_copy(r, stages[i], p).wait_send()
     for r in range(1, heads):
         square_copy(r).wait_send()
     root_copy().wait_send()
@@ -436,7 +448,7 @@
     states = (half, lanes, lanes)
     vmem = pl.BlockSpec(memory_space=pltpu.VMEM)
     smem = pl.BlockSpec(memory_space=pltpu.SMEM)
-    away = pl.BlockSpec(memory_space=pl.ANY)
+    away = pl.BlockSpec(memory_space=pltpu.MemorySpace.HBM)
     f32 = jnp.float32
     dma = pltpu.SemaphoreType.DMA
     return pl.pallas_call(
@@ -474,8 +486,8 @@
             pltpu.VMEM(slots, f32),
             dma((2 + line_bits,)),
             dma((2 + line_bits,)),
-            dma((heads,)),
-            dma((heads,)),
+            dma((heads, PIECES)),
+            dma((heads, PIECES)),
             dma((heads - 1,)),
             dma((heads - 1,)),
             dma((1,)),

time: 93.9 us -> 94.4 us (level)
  no operation moved by 1% of the time
where the time goes in v4:
time: 94.4 us; the launch traced here: 94.1 us
  Pallas kernels  89.8 us (95%)
  local copies, waits for them, and re-layouts  3.74 us (4%)
    pallas_call x1, Pallas kernels, body(): pl.pallas_call(functools.partial(kernel, line, heads), out_shape=(jax.Sha...  89.8 us
    unnamed x2, local copies, waits for them, and re-layouts  3.74 us

profile of v4, /device:TPU:0, one launch (start us, length us, event | category | flops | bytes accessed | tf_op | source)
XLA Modules:
  0.0 94.1 jit_solution(14602117897808477291)
XLA Ops:
  0.6 89.8 %shard_map.68 = (bf16[512,512]{1,0:T(8,128)(2,1)}, f32[256,512]{1,0:T(8,128)}) custom-call(bf16[512,512]{1,0:T(8,128)(2,1)} %q_in.1, bf16[512,512]{1,0:T(8,128)(2,1)} %k_in.1, bf16[512,512]{1,0:T(8,128)(2,1)} %v_in.1, s32[4,20]{1,0:T(4,128)} %level_ref.1, bf16[512,2048]{1,0:T(8,128)(2,1)} %grad_in.1), custom_call_target="tpu_custom_call" | custom-call | tf_op jit(solution)/shard_map/pallas_call | solution.py:454
  90.4 1.9 %copy.9 = bf16[512,512]{1,0:T(8,128)(2,1)} copy(bf16[512,512]{1,0:T(8,128)(2,1)} %get-tuple-element.4) | data formatting | bytes 1048576
  92.3 1.9 %copy.10 = f32[256,512]{1,0:T(8,128)} copy(f32[256,512]{1,0:T(8,128)} %get-tuple-element.5) | data formatting | bytes 1048576
